TPU v7x, 32 devices: a whole 2x2x4 slice. The times are simulated.
32 devices in a mesh: tm: 2 (over core), rows: 16 (over z, y, x).
Axes of the slice: x: 2, y: 2, z: 4, core: 2. Of those that a mesh axis runs over, the one named last changes fastest.
Arguments:
- tiles: bfloat16 [2, 128, 128, 128], P('tm', 'rows'), may hold values from -0.125 to 0.125
- tile_cols: int32 [2, 128], P('tm', 'rows'), may hold values from 0 to 15, as said below
- tile_count: int32 [2, 16], P('tm', 'rows'), may hold values from 4 to 8, as said below
- start_right: bfloat16 [2, 2048, 256], P('tm', 'rows'), may hold values from -48 to 48
Outputs:
- left_embed: float32 [2048, 256], P('rows')
- right_embed: float32 [2, 2048, 256], P('tm', 'rows')
Inputs may be any that keep to these rules, and one draw needn't show every extreme that they name: `tile_cols`: within one row block of one snapshot the 8 slots name distinct column blocks. `tile_count`: some row block of some snapshot has all 8 slots live in every draw.
All inputs are finite; a program needn't handle non-finite values.
Results may differ from a plain program's by a relative error of at most 0.0027.
Values may be sent and summed in bfloat16 or wider, within the bound.
A program may use at most 64 MiB of HBM per device.

v0:
```python
import math
import jax
import jax.numpy as jnp
from jax import lax
from jax.sharding import PartitionSpec as P

BLOCK = 128
COLS = 256


def orthonormal(values, gram, total):
    factor = jnp.linalg.cholesky(gram)
    solved = lax.linalg.triangular_solve(
        factor, values, left_side=False, lower=True, transpose_a=True
    )
    return solved * math.sqrt(total)


def gram_of(values):
    return jnp.dot(values.T, values, precision=lax.Precision.HIGHEST)


def on_device(tiles, tile_cols, tile_count, start_right):
    nrows = lax.axis_size("rows")
    nsnaps = lax.axis_size("tm")
    nodes = BLOCK * nrows
    my_tiles = tiles[0]
    columns = tile_cols[0]
    slot_total = my_tiles.shape[0]
    live = jnp.arange(slot_total, dtype=jnp.int32) < tile_count[0, 0]
    masked = jnp.where(live[:, None, None], my_tiles, jnp.zeros_like(my_tiles))
    onehot = (
        (columns[:, None] == jnp.arange(nrows, dtype=jnp.int32)[None, :]) & live[:, None]
    ).astype(jnp.bfloat16)
    outgoing = jnp.einsum(
        "sc,sij->cij", onehot, my_tiles, preferred_element_type=jnp.float32
    ).astype(jnp.bfloat16)
    incoming = lax.all_to_all(outgoing, "rows", split_axis=0, concat_axis=0, tiled=True)
    current = start_right[0]
    whole = lax.all_gather(current, "rows", axis=0, tiled=True)
    picked = whole.reshape(nrows, BLOCK, COLS)[columns]
    partial_value = jnp.einsum("sij,sjk->ik", masked, picked, preferred_element_type=jnp.float32)
    summed = lax.psum(partial_value, "tm")
    gram = lax.psum(gram_of(summed), "rows")
    left_embed = orthonormal(summed, gram, nodes)
    basis = lax.all_gather(left_embed.astype(jnp.bfloat16), "rows", axis=0, tiled=True)
    image = jnp.einsum(
        "rij,rik->jk",
        incoming,
        basis.reshape(nrows, BLOCK, COLS),
        preferred_element_type=jnp.float32,
    )
    rgram = lax.psum(gram_of(image), ("tm", "rows"))
    right_embed = orthonormal(image, rgram, nodes * nsnaps)
    return (left_embed, right_embed[None])


def solution(mesh):
    placed = (P("tm", "rows", None, None), P("tm", "rows"), P("tm", "rows"), P("tm", "rows", None))
    return jax.shard_map(
        on_device,
        mesh=mesh,
        in_specs=placed,
        out_specs=(P("rows", None), P("tm", "rows", None)),
        check_vma=False,
    )
```

profile of v0, /device:TPU:0, one launch (start us, length us, event | category | flops | bytes accessed | tf_op | source)
XLA Modules:
  0.0 516.3 jit_solution(13948619918923073705)
XLA Ops:
  7.2 0.7 all-gather.6.cloned.1.call-update
  8.6 0.6 copy-done.4
  9.3 59.5 %all-gather.6.cloned.1.call-done = bf16[1,2048,256]{2,1,0:T(8,128)(2,1)} async-done(((bf16[1,128,256]{2,1,0:T(8,128)(2,1)}), bf16[1,2048,256]{2,1,0:T(8,128)(2,1)}) %all-gather.6.cloned.1.call-update) | async-done | bytes 1048592 | tf_op jit(solution)/shard_map/all_gather | solution.py:40
  68.8 1.8 gather_fusion
  70.6 0.9 convolution_bitcast_fusion
  71.6 16.8 %all-reduce.5.cloned.1.call-done = f32[128,256]{1,0:T(8,128)} async-done(((f32[128,256]{1,0:T(8,128)}), f32[128,256]{1,0:T(8,128)}) %all-reduce.5.cloned.1.call-update) | async-done | bytes 131088 | tf_op jit(solution)/shard_map/psum | solution.py:43
  88.5 2.1 fusion.33
  90.6 111.0 %all-reduce.7.cloned.1.call-done = f32[256,256]{0,1:T(8,128)} async-done(((f32[256,256]{0,1:T(8,128)}), f32[256,256]{0,1:T(8,128)}) %all-reduce.7.cloned.1.call-update) | async-done | bytes 262160 | tf_op jit(solution)/shard_map/psum | solution.py:44
  201.6 1.1 copy.7
  202.8 11.7 %cholesky.130 = f32[128,128]{1,0:T(8,128)S(1)} custom-call(f32[128,128]{1,0:T(8,128)S(1)} %cholesky.194), custom_call_target="Cholesky" | custom-call | tf_op jit(solution)/shard_map/jit(cholesky)/cholesky | solution.py:12
  214.6 9.8 %custom-call.13 = f32[1,128,128]{1,2,0:T(8,128)S(1)} custom-call(f32[1,128,128]{2,1,0:T(8,128)S(1)} %get-tuple-element.51), custom_call_target="InvertDiagBlocksLowerTriangular" | custom-call | tf_op jit(solution)/shard_map/jit(cholesky)/cholesky | solution.py:12
  224.9 11.7 %cholesky.147 = f32[128,128]{1,0:T(8,128)S(1)} custom-call(f32[128,128]{1,0:T(8,128)S(1)} %convolution_subtract_fusion.3), custom_call_target="Cholesky" | custom-call | tf_op jit(solution)/shard_map/jit(cholesky)/cholesky | solution.py:12
  236.7 0.7 compare_reduce_fusion.2
  238.8 4.2 while.4
  239.0 0.6 fusion.52
  239.5 1.4 bitcast_dynamic-update-slice_fusion.4
  241.0 0.6 fusion.52
  241.5 1.4 bitcast_dynamic-update-slice_fusion.4
  242.9 19.7 %custom-call.14 = f32[2,128,128]{1,2,0:T(8,128)S(1)} custom-call(f32[2,128,128]{2,1,0:T(8,128)S(1)} %get-tuple-element.18), custom_call_target="InvertDiagBlocksLowerTriangular" | custom-call | tf_op jit(solution)/shard_map/triangular_solve/custom-call.0 | solution.py:13
  262.6 0.3 fusion.16
  262.9 0.3 convolution_subtract_fusion.2
  263.2 0.3 fusion.14
  263.5 0.6 fusion.30
  264.2 0.4 fusion.2
  264.6 1.2 copy.15
  265.8 4.6 all-to-all-start
  270.5 45.9 %all-gather.4.cloned.1.call-done = bf16[2048,256]{0,1:T(8,128)(2,1)} async-done(((bf16[128,256]{0,1:T(8,128)(2,1)}), bf16[2048,256]{0,1:T(8,128)(2,1)}) %all-gather.4.cloned.1.call-update) | async-done | bytes 1048592 | tf_op jit(solution)/shard_map/all_gather | solution.py:46
  316.4 1.5 copy.17
  317.9 0.3 convolution_bitcast_fusion.1
  318.2 1.1 fusion.34
  319.3 0.8 copy.11
  320.1 126.4 %all-reduce.9.cloned.1.call-done = f32[256,256]{0,1:T(8,128)} async-done(((f32[256,256]{0,1:T(8,128)}), f32[256,256]{0,1:T(8,128)}) %all-reduce.9.cloned.1.call-update) | async-done | bytes 262160 | tf_op jit(solution)/shard_map/psum | solution.py:53
  446.5 1.1 copy.10
  447.7 11.7 %cholesky.164 = f32[128,128]{1,0:T(8,128)S(1)} custom-call(f32[128,128]{1,0:T(8,128)S(1)} %cholesky.197), custom_call_target="Cholesky" | custom-call | tf_op jit(solution)/shard_map/jit(cholesky)/cholesky | solution.py:12
  459.5 9.8 %custom-call.15 = f32[1,128,128]{1,2,0:T(8,128)S(1)} custom-call(f32[1,128,128]{2,1,0:T(8,128)S(1)} %get-tuple-element.47), custom_call_target="InvertDiagBlocksLowerTriangular" | custom-call | tf_op jit(solution)/shard_map/jit(cholesky)/cholesky | solution.py:12
  469.8 11.7 %cholesky.181 = f32[128,128]{1,0:T(8,128)S(1)} custom-call(f32[128,128]{1,0:T(8,128)S(1)} %convolution_subtract_fusion.1), custom_call_target="Cholesky" | custom-call | tf_op jit(solution)/shard_map/jit(cholesky)/cholesky | solution.py:12
  481.6 0.7 compare_reduce_fusion
  482.2 0.6 compare_reduce_fusion.1
  484.2 4.0 while.5
  484.2 0.6 fusion.53
  484.8 1.4 bitcast_dynamic-update-slice_fusion.5
  486.2 0.6 fusion.53
  486.8 1.4 bitcast_dynamic-update-slice_fusion.5
  488.2 19.9 %custom-call.16 = f32[2,128,128]{1,2,0:T(8,128)S(1)} custom-call(f32[2,128,128]{2,1,0:T(8,128)S(1)} %get-tuple-element.19), custom_call_target="InvertDiagBlocksLowerTriangular" | custom-call | tf_op jit(solution)/shard_map/triangular_solve/custom-call.0 | solution.py:13
  508.1 0.3 fusion.10
  508.4 0.3 convolution_subtract_fusion
  508.7 0.3 fusion.8
  509.0 0.8 copy.12
  (47 shorter events, 1.7 us)
Async XLA Ops:
  7.2 61.6 %all-gather.6.cloned.1.call-start = ((), (), s32[]{:S(2)}) async-start(), calls=%async_computation.5 | async-start | bytes 1114112 | tf_op jit(solution)/shard_map/all_gather | solution.py:40
  7.9 80.6 %all-reduce.5.cloned.1.call-start = ((), (), s32[]{:S(2)}) async-start(), calls=%async_computation.1 | async-start | bytes 262144 | tf_op jit(solution)/shard_map/psum | solution.py:43
  8.6 0.7 copy-start.4
  68.8 1.9 copy-start.1
  71.6 130.0 %all-reduce.7.cloned.1.call-start = ((), (), s32[]{:S(2)}) async-start(), calls=%async_computation.2 | async-start | bytes 524288 | tf_op jit(solution)/shard_map/psum | solution.py:44
  90.6 225.8 %all-gather.4.cloned.1.call-start = ((), (), s32[]{:S(2)}) async-start(), calls=%async_computation.3 | async-start | bytes 1114112 | tf_op jit(solution)/shard_map/all_gather | solution.py:46
  201.6 1.2 copy-start.2
  238.7 23.9 %copy-start = (f32[128,256]{1,0:T(8,128)S(1)}, f32[128,256]{1,0:T(8,128)}, u32[]{:S(2)}) copy-start(f32[128,256]{1,0:T(8,128)} %all-reduce.5.cloned.1.call-done) | copy-start | bytes 393220
  265.8 52.0 %all-to-all-start = ((bf16[16,128,128]{1,2,0:T(8,128)(2,1)}), bf16[16,128,128]{1,2,0:T(8,128)(2,1)S(1)}, u32[]{:S(2)}, u32[]{:S(2)}) async-start(bf16[16,128,128]{1,2,0:T(8,128)(2,1)} %copy.15), calls=%async_computation | async-start | bytes 1048576 | tf_op jit(solution)/shard_map/all_to_all | solution.py:38
  270.5 176.0 %all-reduce.9.cloned.1.call-start = ((), (), s32[]{:S(2)}) async-start(), calls=%async_computation.4 | async-start | bytes 524288 | tf_op jit(solution)/shard_map/psum | solution.py:53
  446.5 1.2 copy-start.3
Sparse Core Ops, SparseCore 0:
  10.8 57.9 all-gather.5
  71.7 16.7 all-reduce.4
  93.7 107.8 all-reduce.6
  264.3 52.0 all-gather.3
  322.7 123.8 all-reduce.8
where the time goes:
time: 517 us; the launch traced here: 516 us
  waiting for transfers between devices  360 us (70%)
  other arithmetic  109 us (21%)
  between operations  17.3 us (3%)
  local copies, waits for them, and re-layouts  17 us (3%)
  matrix products  7.52 us (1%)
    psum x1, waiting for transfers between devices, on_device(): rgram = lax.psum(gram_of(image), ('tm', 'rows'))  126 us
    psum x1, waiting for transfers between devices, on_device(): gram = lax.psum(gram_of(summed), 'rows')  111 us
    another operation x13, other arithmetic, orthonormal(): factor = jnp.linalg.cholesky(gram)  68.6 us
    all_gather x1, waiting for transfers between devices, on_device(): whole = lax.all_gather(current, 'rows', axis=0, tiled=True)  59.5 us
    all_gather x1, waiting for transfers between devices, on_device(): lax.all_gather(left_embed.astype(jnp.bfloat16), 'rows', axis=0, tiled=True)  45.9 us
    another operation x5, other arithmetic, orthonormal(): lax.linalg.triangular_solve(factor, values, left_side=False, lower=True,...  39.6 us
    psum x1, waiting for transfers between devices, on_device(): summed = lax.psum(partial_value, 'tm')  16.8 us
  transfers between devices with their start and end apart: 6, of which 5 were waited for; matrix products, arithmetic and copies ran while one was open for 1% of the time, Pallas kernels for 0%

commit v1 on v0

--- a/solution.py
+++ b/solution.py
@@ -50,7 +50,7 @@
         basis.reshape(nrows, BLOCK, COLS),
         preferred_element_type=jnp.float32,
     )
-    rgram = lax.psum(gram_of(image), ("tm", "rows"))
+    rgram = jnp.sum(lax.all_gather(gram_of(image), ("tm", "rows")), axis=0)
     right_embed = orthonormal(image, rgram, nodes * nsnaps)
     return (left_embed, right_embed[None])
 

time: 517 us -> 474 us (0.917)
  waiting for transfers between devices: 360 us -> 309 us
  other arithmetic: 109 us -> 115 us
    psum x1 -> x0, waiting for transfers between devices: 126 us -> none  [on_device(): rgram = lax.psum(gram_of(image), ('tm', 'rows'))]
    all_gather x0 -> x1, waiting for transfers between devices: none -> 75.9 us  [on_device(): rgram = jnp.sum(lax.all_gather(gram_of(image), ('tm', 'rows')), axis=0)]
where the time goes in v1:
time: 474 us; the launch traced here: 473 us
  waiting for transfers between devices  309 us (65%)
  other arithmetic  115 us (24%)
  between operations  17.4 us (4%)
  local copies, waits for them, and re-layouts  15.5 us (3%)
  matrix products  11.1 us (2%)
  starting transfers between devices  4.83 us (1%)
    psum x1, waiting for transfers between devices, on_device(): gram = lax.psum(gram_of(summed), 'rows')  111 us
    all_gather x1, waiting for transfers between devices, on_device(): rgram = jnp.sum(lax.all_gather(gram_of(image), ('tm', 'rows')), axis=0)  75.9 us
    another operation x13, other arithmetic, orthonormal(): factor = jnp.linalg.cholesky(gram)  68.7 us
    all_gather x1, waiting for transfers between devices, on_device(): whole = lax.all_gather(current, 'rows', axis=0, tiled=True)  59.5 us
    all_gather x1, waiting for transfers between devices, on_device(): lax.all_gather(left_embed.astype(jnp.bfloat16), 'rows', axis=0, tiled=True)  45.1 us
    another operation x5, other arithmetic, orthonormal(): lax.linalg.triangular_solve(factor, values, left_side=False, lower=True,...  39.6 us
    psum x1, waiting for transfers between devices, on_device(): summed = lax.psum(partial_value, 'tm')  16.8 us
  transfers between devices with their start and end apart: 6, of which 5 were waited for; matrix products, arithmetic and copies ran while one was open for 1% of the time, Pallas kernels for 0%

profile of v1, /device:TPU:0, one launch (start us, length us, event | category | flops | bytes accessed | tf_op | source)
XLA Modules:
  0.0 472.8 jit_solution(2501527382287820364)
XLA Ops:
  7.2 0.7 all-gather.8.cloned.1.call-update
  8.6 0.7 fusion.27
  9.3 59.5 %all-gather.8.cloned.1.call-done = bf16[1,2048,256]{2,1,0:T(8,128)(2,1)} async-done(((bf16[1,128,256]{2,1,0:T(8,128)(2,1)}), bf16[1,2048,256]{2,1,0:T(8,128)(2,1)}) %all-gather.8.cloned.1.call-update) | async-done | bytes 1048592 | tf_op jit(solution)/shard_map/all_gather | solution.py:40
  68.8 1.8 gather_fusion
  70.6 1.9 convolution_bitcast_fusion
  72.5 16.8 %all-reduce.4.cloned.1.call-done = f32[128,256]{1,0:T(8,128)} async-done(((f32[128,256]{1,0:T(8,128)}), f32[128,256]{1,0:T(8,128)}) %all-reduce.4.cloned.1.call-update) | async-done | bytes 131088 | tf_op jit(solution)/shard_map/psum | solution.py:43
  89.4 2.1 fusion.33
  91.5 111.0 %all-reduce.6.cloned.1.call-done = f32[256,256]{0,1:T(8,128)} async-done(((f32[256,256]{0,1:T(8,128)}), f32[256,256]{0,1:T(8,128)}) %all-reduce.6.cloned.1.call-update) | async-done | bytes 262160 | tf_op jit(solution)/shard_map/psum | solution.py:44
  202.6 1.1 copy.13
  203.7 1.0 fusion.1
  204.7 11.7 %cholesky.130 = f32[128,128]{1,0:T(8,128)S(1)} custom-call(f32[128,128]{1,0:T(8,128)S(1)} %cholesky.194), custom_call_target="Cholesky" | custom-call | tf_op jit(solution)/shard_map/jit(cholesky)/cholesky | solution.py:12
  216.4 9.8 %custom-call.13 = f32[1,128,128]{1,2,0:T(8,128)S(1)} custom-call(f32[1,128,128]{2,1,0:T(8,128)S(1)} %get-tuple-element.53), custom_call_target="InvertDiagBlocksLowerTriangular" | custom-call | tf_op jit(solution)/shard_map/jit(cholesky)/cholesky | solution.py:12
  226.7 11.7 %cholesky.147 = f32[128,128]{1,0:T(8,128)S(1)} custom-call(f32[128,128]{1,0:T(8,128)S(1)} %convolution_subtract_fusion.3), custom_call_target="Cholesky" | custom-call | tf_op jit(solution)/shard_map/jit(cholesky)/cholesky | solution.py:12
  238.5 0.7 compare_reduce_fusion.2
  240.7 4.3 while.4
  240.9 0.6 fusion.52
  241.5 1.4 bitcast_dynamic-update-slice_fusion.4
  242.9 0.6 fusion.52
  243.5 1.4 bitcast_dynamic-update-slice_fusion.4
  245.0 19.7 %custom-call.14 = f32[2,128,128]{1,2,0:T(8,128)S(1)} custom-call(f32[2,128,128]{2,1,0:T(8,128)S(1)} %get-tuple-element.18), custom_call_target="InvertDiagBlocksLowerTriangular" | custom-call | tf_op jit(solution)/shard_map/triangular_solve/custom-call.0 | solution.py:13
  264.7 1.1 fusion.16
  265.8 1.1 convolution_subtract_fusion.2
  266.9 0.3 fusion.14
  267.2 0.6 fusion.30
  267.9 1.4 fusion.2
  269.3 1.3 copy.20
  270.5 4.6 all-to-all-start
  275.2 45.1 %all-gather.6.cloned.1.call-done = bf16[2048,256]{0,1:T(8,128)(2,1)} async-done(((bf16[128,256]{0,1:T(8,128)(2,1)}), bf16[2048,256]{0,1:T(8,128)(2,1)}) %all-gather.6.cloned.1.call-update) | async-done | bytes 1048592 | tf_op jit(solution)/shard_map/all_gather | solution.py:46
  320.3 1.5 copy.21
  321.8 0.3 convolution_bitcast_fusion.1
  322.1 1.1 fusion.34
  323.3 0.8 copy.16
  324.0 75.9 %all-gather.10.cloned.1.call-done = f32[8192,256]{1,0:T(8,128)} async-done(((f32[256,256]{1,0:T(8,128)}), f32[8192,256]{1,0:T(8,128)}) %all-gather.10.cloned.1.call-update) | async-done | bytes 8388624 | tf_op jit(solution)/shard_map/all_gather | solution.py:53
  399.9 3.9 reduce_sum.9
  404.1 11.7 %cholesky.164 = f32[128,128]{1,0:T(8,128)S(1)} custom-call(f32[128,128]{1,0:T(8,128)S(1)} %cholesky.197), custom_call_target="Cholesky" | custom-call | tf_op jit(solution)/shard_map/jit(cholesky)/cholesky | solution.py:12
  415.8 9.8 %custom-call.15 = f32[1,128,128]{1,2,0:T(8,128)S(1)} custom-call(f32[1,128,128]{2,1,0:T(8,128)S(1)} %get-tuple-element.49), custom_call_target="InvertDiagBlocksLowerTriangular" | custom-call | tf_op jit(solution)/shard_map/jit(cholesky)/cholesky | solution.py:12
  426.1 11.7 %cholesky.181 = f32[128,128]{1,0:T(8,128)S(1)} custom-call(f32[128,128]{1,0:T(8,128)S(1)} %convolution_subtract_fusion.1), custom_call_target="Cholesky" | custom-call | tf_op jit(solution)/shard_map/jit(cholesky)/cholesky | solution.py:12
  437.8 0.6 compare_reduce_fusion.1
  438.5 0.7 compare_reduce_fusion
  440.6 4.1 while.5
  440.7 0.6 fusion.53
  441.2 1.4 bitcast_dynamic-update-slice_fusion.5
  442.7 0.6 fusion.53
  443.3 1.4 bitcast_dynamic-update-slice_fusion.5
  444.7 19.9 %custom-call.16 = f32[2,128,128]{1,2,0:T(8,128)S(1)} custom-call(f32[2,128,128]{2,1,0:T(8,128)S(1)} %get-tuple-element.19), custom_call_target="InvertDiagBlocksLowerTriangular" | custom-call | tf_op jit(solution)/shard_map/triangular_solve/custom-call.0 | solution.py:13
  464.9 0.3 convolution_subtract_fusion
  465.2 0.3 fusion.8
  465.6 0.8 copy.17
  (38 shorter events, 2.1 us)
Async XLA Ops:
  7.2 61.6 %all-gather.8.cloned.1.call-start = ((), (), s32[]{:S(2)}) async-start(), calls=%async_computation.4 | async-start | bytes 1114112 | tf_op jit(solution)/shard_map/all_gather | solution.py:40
  7.9 81.5 %all-reduce.4.cloned.1.call-start = ((), (), s32[]{:S(2)}) async-start(), calls=%async_computation.1 | async-start | bytes 262144 | tf_op jit(solution)/shard_map/psum | solution.py:43
  72.5 130.1 %all-reduce.6.cloned.1.call-start = ((), (), s32[]{:S(2)}) async-start(), calls=%async_computation.2 | async-start | bytes 524288 | tf_op jit(solution)/shard_map/psum | solution.py:44
  91.5 228.9 %all-gather.6.cloned.1.call-start = ((), (), s32[]{:S(2)}) async-start(), calls=%async_computation.3 | async-start | bytes 1114112 | tf_op jit(solution)/shard_map/all_gather | solution.py:46
  270.5 51.3 %all-to-all-start = ((bf16[16,128,128]{1,2,0:T(8,128)(2,1)}), bf16[16,128,128]{1,2,0:T(8,128)(2,1)S(1)}, u32[]{:S(2)}, u32[]{:S(2)}) async-start(bf16[16,128,128]{1,2,0:T(8,128)(2,1)} %copy.20), calls=%async_computation | async-start | bytes 1048576 | tf_op jit(solution)/shard_map/all_to_all | solution.py:38
  275.2 124.8 %all-gather.10.cloned.1.call-start = ((), (), s32[]{:S(2)}) async-start(), calls=%async_computation.5 | async-start | bytes 8650752 | tf_op jit(solution)/shard_map/all_gather | solution.py:53
Sparse Core Ops, SparseCore 0:
  10.8 57.9 all-gather.7
  72.6 16.7 all-reduce.3
  94.6 107.9 all-reduce.5
  268.0 52.2 all-gather.5
  323.5 76.4 all-gather.9
